TPU v7x, 128 devices: a whole 4x4x4 slice. The times are simulated.
128 devices in a mesh: lat: 32 (over y, x, core), lev: 4 (over z).
Axes of the slice: x: 4, y: 4, z: 4, core: 2. Of those that a mesh axis runs over, the one named last changes fastest.
Arguments:
- adjoint_grid: bfloat16 [32, 64, 2, 5136], P('lev', 'lat'), may hold values from -6 to 6
- lower_diffusion: float32 [32, 64, 5136], P(None, 'lat', 'lev'), may hold values from 0.2 to 20
- upper_diffusion: float32 [32, 64, 5136], P(None, 'lat', 'lev'), may hold values from 0.2 to 20
- row_lengths: int32 [32], replicated, may hold values from 1280 to 5136, as said below
- wave_order: int32 [1280], replicated, may hold values from 0 to 1279, each once
Outputs:
- spectral: float32 [1280, 2, 2, 32, 64], P('lat', None, None, 'lev')
Inputs may be any that keep to these rules, and one draw needn't show every extreme that they name: `row_lengths`: lengths never fall from pole to equator; the first is 1280 and the last 5136.
All inputs are finite; a program needn't handle non-finite values.
Results may differ from a plain program's by a relative error of at most 0.0037.
Values may be sent and summed in bfloat16 or wider, within the bound.
No kernel may reach another device: no remote copies, remote signals or barrier semaphores. Data moves between devices by JAX's collectives and lax.ppermute only.
A program may use at most 128 MiB of HBM per device.

v0:
```python
import math

import jax
import jax.numpy as jnp
from jax import lax
from jax.experimental import pallas as pl
from jax.experimental.pallas import tpu as pltpu
from jax.sharding import PartitionSpec as P

LANE = 128
DEEP = 256
LIMIT = pltpu.CompilerParams(vmem_limit_bytes=24 << 20)
TWO_PI = 6.283185307179586
VMEM = pl.BlockSpec(memory_space=pltpu.VMEM)
ANY = pl.BlockSpec(memory_space=pl.ANY)


def sizes(points, lev_count):
    block = points // lev_count
    step = block // LANE * LANE
    window = step + LANE
    return block, step, window


def pack_kernel(lev_count, shifts, x_hbm, lengths_hbm, *refs):
    outs, (limit_ref, x_ref, lengths_ref, sems) = refs[: len(shifts)], refs[len(shifts) :]
    levels, rows, fields, points = x_ref.shape
    _, step, _ = sizes(points, lev_count)
    last = points - lev_count * step
    me = lax.axis_index("lev")
    pairs = [(x_hbm.at[level], x_ref.at[level]) for level in range(levels)]
    pairs += [(lengths_hbm, lengths_ref)]
    copies = [pltpu.make_async_copy(source, target, sems.at[i]) for i, (source, target) in enumerate(pairs)]
    for copy in copies:
        copy.start()
    pieces = len(copies) - 1
    for piece in range(pieces):
        copies[piece].wait()
        some = range(levels * piece // pieces, levels * (piece + 1) // pieces)
        for shift, out in zip(shifts, outs):
            to = lax.rem(me + shift, lev_count)
            base = pl.multiple_of(to * step, LANE)
            for level in some:
                for row in range(rows):
                    low = fields * (rows * level + row)
                    out[low : low + fields, :step] = x_ref[level, row, :, pl.ds(base, step)]
    for shift, out in zip(shifts, outs):
        to = lax.rem(me + shift, lev_count)

        @pl.when(to < lev_count - 1)
        def _():
            tail = pl.multiple_of(to * step + step, LANE)
            for level in range(levels):
                for row in range(rows):
                    low = fields * (rows * level + row)
                    out[low : low + fields, step:] = x_ref[level, row, :, pl.ds(tail, LANE)]

        @pl.when(to == lev_count - 1)
        def _():
            for level in range(levels):
                for row in range(rows):
                    low = fields * (rows * level + row)
                    out[low : low + fields, step : step + last] = x_ref[level, row, :, lev_count * step :]

    copies[-1].wait()
    first = rows * lax.axis_index("lat")
    for row in range(rows):
        whole = lengths_ref[lax.rem(first + row, lengths_ref.shape[0])]
        limit_ref[row : row + 1, :] = jnp.full((1, LANE), whole, jnp.int32)


def turn(multiple, length):
    inverse = 1.0 / length
    rest = multiple - jnp.floor(multiple * inverse) * length
    rest = jnp.where(rest < 0.0, rest + length, rest)
    rest = jnp.where(rest >= length, rest - length, rest)
    quarter = jnp.floor(4.0 * rest * inverse + 0.5)
    angle = (4.0 * rest - quarter * length) * ((TWO_PI / 4.0) * inverse)
    square = angle * angle
    sine = angle + angle * square * (-1.6666654611e-1 + square * (8.3321608736e-3 + square * -1.9515295891e-4))
    cosine = 1.0 - 0.5 * square + square * square * (
        4.166664568298827e-2 + square * (-1.388731625493765e-3 + square * 2.443315711809948e-5)
    )
    odd = (quarter == 1.0) | (quarter == 3.0)
    real = jnp.where(odd, sine, cosine)
    imag = jnp.where(odd, cosine, sine)
    real = jnp.where((quarter == 1.0) | (quarter == 2.0), -real, real)
    imag = jnp.where((quarter == 2.0) | (quarter == 3.0), imag, -imag)
    return real, imag


def table_kernel(limit_ref, wave_ref, after_ref, fine_ref, coarse_ref):
    rows = fine_ref.shape[0]
    waves = wave_ref.shape[1]
    wave = wave_ref[...].astype(jnp.float32)
    coarse_rows = coarse_ref.shape[2]
    small = lax.broadcasted_iota(jnp.int32, (16, 1), 0).astype(jnp.float32)
    blocks = lax.broadcasted_iota(jnp.int32, (coarse_rows, 1), 0).astype(jnp.float32)
    for row in range(rows):
        length = limit_ref[row : row + 1, :1].astype(jnp.float32)
        near_real, near_imag = turn(wave * small, length)
        far_real, far_imag = turn(wave * (16.0 * small), length)
        for part in range(16):
            one_real = far_real[part : part + 1]
            one_imag = far_imag[part : part + 1]
            low = 16 * part
            fine_ref[row, low : low + 16, :waves] = (near_real * one_real - near_imag * one_imag).astype(jnp.bfloat16)
            fine_ref[row, low : low + 16, waves:] = (near_real * one_imag + near_imag * one_real).astype(jnp.bfloat16)
        real, imag = turn(wave * (float(DEEP) * blocks), length)
        scale = jnp.where(2.0 * wave < length, 1.0 / jnp.sqrt(length), 0.0)
        coarse_ref[row, 0] = real * scale
        coarse_ref[row, 1] = imag * scale


def factor_kernel(
    lev_count, points, fields, lower_hbm, upper_hbm, after_ref, first_ref, second_ref, third_ref, lower_ref, upper_ref, sems
):
    block, step, _ = sizes(points, lev_count)
    levels, rows = lower_ref.shape[:2]
    copies = [
        pltpu.make_async_copy(lower_hbm, lower_ref, sems.at[0]),
        pltpu.make_async_copy(upper_hbm, upper_ref, sems.at[1]),
    ]
    for copy in copies:
        copy.start()
    for copy in copies:
        copy.wait()
    me_lev = lax.axis_index("lev")
    own = levels // lev_count
    ratio = None
    for level in range(levels):
        upper = upper_ref[level]
        if level == 0:
            pivot = 1.0 + upper
            above = jnp.zeros_like(upper)
        else:
            diagonal = 1.0 + lower_ref[level]
            if level < levels - 1:
                diagonal = diagonal + upper
            above = upper_ref[level - 1]
            pivot = diagonal + above * ratio
        inverse = 1.0 / pivot
        if level < levels - 1:
            ratio = -lower_ref[level + 1] * inverse
        else:
            ratio = jnp.zeros_like(inverse)
        chunk, inner = divmod(level, own)
        for out, value in ((first_ref, inverse), (second_ref, above * inverse), (third_ref, ratio)):
            for row in range(rows):
                low = fields * (rows * inner + row)
                out[chunk, low : low + fields, :block] = jnp.broadcast_to(value[row : row + 1], (fields, block))
    for out in (first_ref, second_ref, third_ref):
        for chunk in range(out.shape[0]):
            out[chunk] = pltpu.roll(out[chunk], me_lev * (block - step), 1)


def solve_kernel(lev_count, points, fields, limit_ref, first_ref, second_ref, third_ref, *refs):
    block, step, window = sizes(points, lev_count)
    sources, outs, work, done = refs[:lev_count], refs[lev_count : 2 * lev_count], refs[-2], refs[-1]
    rows, members = done.shape[1:3]
    own = members // fields
    levels = lev_count * own
    wide = rows * fields
    me_lev = lax.axis_index("lev")
    for shift, source in enumerate(sources):
        chunk = lax.rem(me_lev + lev_count - shift, lev_count)
        work[chunk] = source[...].astype(jnp.float32)
    lane = lax.broadcasted_iota(jnp.int32, (1, window), 1)
    offset = me_lev * (block - step)
    inside = []
    for row in range(rows):
        whole = limit_ref[row : row + 1, :1]
        inside.append((lane >= offset) & (lane < offset + block) & (lane + me_lev * step < whole))
    part = None
    for level in range(levels):
        chunk, inner = divmod(level, own)
        at = (chunk, slice(wide * inner, wide * (inner + 1)))
        value = work[at] * first_ref[at]
        part = value if part is None else value + second_ref[at] * part
        work[at] = part
    current = None
    for level in range(levels - 1, -1, -1):
        chunk, inner = divmod(level, own)
        at = (chunk, slice(wide * inner, wide * (inner + 1)))
        current = work[at] if current is None else work[at] - third_ref[at] * current
        for row in range(rows):
            done[chunk, row, fields * inner : fields * (inner + 1)] = current[fields * row : fields * (row + 1)]
    for shift, out in enumerate(outs):
        chunk = lax.rem(me_lev + shift, lev_count)
        for row in range(rows):
            out[row] = jnp.where(inside[row], done[chunk, row], 0.0).astype(jnp.bfloat16)


def blocks_sum(fine_ref, coarse_ref, row, tile, main, places, real, imag):
    waves = fine_ref.shape[2] // 2
    members = main.shape[0] // len(places)
    low = DEEP * tile
    all_cos = jnp.dot(main, fine_ref[row, :, low : low + DEEP], preferred_element_type=jnp.float32)
    all_sin = jnp.dot(main, fine_ref[row, :, waves + low : waves + low + DEEP], preferred_element_type=jnp.float32)
    for piece, place in enumerate(places):
        pos = members * piece
        y_cos, y_sin = all_cos[pos : pos + members], all_sin[pos : pos + members]
        c = coarse_ref[row, 0, pl.ds(place, 1), low : low + DEEP]
        s = coarse_ref[row, 1, pl.ds(place, 1), low : low + DEEP]
        real = real + (y_cos * c - y_sin * s)
        imag = imag + (y_sin * c + y_cos * s)
    return real, imag


def origin_of(shift, count):
    return lax.rem(lax.axis_index("lev") + count - shift, count)


def early_kernel(lev_count, points, shifts, fine_ref, coarse_ref, *refs):
    _, step, _ = sizes(points, lev_count)
    sources, spectra = refs[:-1], refs[-1]
    rows, _, _, members, _ = spectra.shape
    waves = fine_ref.shape[2] // 2
    per = step // DEEP
    places = [per * origin_of(shift, lev_count) + a for shift in shifts for a in range(1, per)]
    for row in range(rows):
        main = jnp.concatenate(
            [source[row, :, DEEP * a : DEEP * (a + 1)] for source in sources for a in range(1, per)], axis=0
        )
        for tile in range(waves // DEEP):
            zero = jnp.zeros((members, DEEP), jnp.float32)
            sums = blocks_sum(fine_ref, coarse_ref, row, tile, main, places, zero, zero)
            for half in range(DEEP // LANE):
                for part, value in enumerate(sums):
                    spectra[row, part, tile * (DEEP // LANE) + half] = value[:, LANE * half : LANE * (half + 1)]


def fourier_kernel(lev_count, points, early, order, fine_ref, coarse_ref, begun_ref, *refs):
    block, step, _ = sizes(points, lev_count)
    sources, out_ref, spectra, turned = refs[:lev_count], refs[-3], refs[-2], refs[-1]
    rows = fine_ref.shape[0]
    waves = fine_ref.shape[2] // 2
    per = step // DEEP
    final = [origin_of(shift, lev_count) == lev_count - 1 for shift in range(lev_count)]
    places = []
    for shift in range(lev_count):
        places += [per * origin_of(shift, lev_count) + a for a in range(1 if shift in early else per)]
    places.append(per * lev_count)
    for row in range(rows):
        tails = [source[row, :, step:] for source in sources]
        none = jnp.zeros_like(tails[0])
        pieces = []
        for shift, source in enumerate(sources):
            before = (shift + 1) % lev_count
            first = source[row, :, :LANE] + jnp.where(final[before], none, tails[before])
            pieces.append(jnp.concatenate([first, source[row, :, LANE:DEEP]], axis=1))
            if shift not in early:
                pieces += [source[row, :, DEEP * a : DEEP * (a + 1)] for a in range(1, per)]
        beyond = none
        for shift in range(lev_count):
            beyond = jnp.where(final[shift], tails[shift], beyond)
        pieces.append(jnp.concatenate([beyond, none], axis=1))
        main = jnp.concatenate(pieces, axis=0)
        for tile in range(waves // DEEP):
            halves = [tile * (DEEP // LANE) + half for half in range(DEEP // LANE)]
            begun = [jnp.concatenate([begun_ref[row, part, at] for at in halves], axis=1) for part in range(2)]
            sums = blocks_sum(fine_ref, coarse_ref, row, tile, main, places, *begun)
            for half, at in enumerate(halves):
                for part, value in enumerate(sums):
                    spectra[row, part, at] = value[:, LANE * half : LANE * (half + 1)]
    for tile in range(waves // LANE):
        low = LANE * tile
        pieces = []
        for row in range(rows):
            one = [
                spectra[row, c, tile, pl.ds(field, spectra.shape[3] // 2, stride=2), :] for c in range(2) for field in range(2)
            ]
            pieces += one + one
        turned[low : low + LANE, :] = jnp.concatenate(pieces, axis=0).T
    parts, groups, inner = out_ref.shape[:3]
    high = groups * inner
    slots = waves // parts
    lane = lax.broadcasted_iota(jnp.int32, (high, LANE), 1)
    left = lax.rem(lane, LANE // 2) < LANE // 4
    for place, part in enumerate(order):
        top = turned[slots * part : slots * part + high, :]
        low = turned[slots * part + high : slots * (part + 1), :]
        block = jnp.where(left, top, low).astype(jnp.bfloat16)
        for group in range(groups):
            out_ref[place, group] = block[inner * group : inner * (group + 1)]


def pair_kernel(order, in_ref, out_ref, work, made, sems):
    parts, groups, inner = in_ref.shape[:3]
    high = groups * inner
    slots = out_ref.shape[0]
    grid_rows = out_ref.shape[4]
    rows = grid_rows // parts
    for place, part in enumerate(order):
        for group in range(groups):
            low = high * part + inner * group
            work[low : low + inner, :] = in_ref[place, group].astype(jnp.float32)
    source = lax.broadcasted_iota(jnp.int32, (parts, grid_rows), 0)
    target = lax.broadcasted_iota(jnp.int32, (parts, grid_rows), 1)
    half = grid_rows // 2
    mixes = []
    for row in range(rows):
        place = rows * source + row
        same = lax.rem(place, half) == lax.rem(target, half)
        sign = jnp.where((target >= half) & (place >= half), -1.0, 1.0)
        mixes.append(jnp.where(same, sign, 0.0).astype(jnp.bfloat16))
    half_lanes = LANE // 2
    quarter = half_lanes // 2
    group = 4
    copies = []
    for begin in range(0, high, group):
        turned = [
            work[pl.ds(slot, parts, stride=high), :].T.astype(jnp.bfloat16) for slot in range(begin, begin + group)
        ]
        above = jnp.concatenate([block[:half_lanes] for block in turned], axis=0)
        below = jnp.concatenate([block[half_lanes:] for block in turned], axis=0)
        result = jnp.dot(above, mixes[0], preferred_element_type=jnp.float32)
        result = result + jnp.dot(below, mixes[1], preferred_element_type=jnp.float32)
        for slot in range(group):
            both = result[half_lanes * slot : half_lanes * (slot + 1)]
            made[begin + slot] = both[:quarter].reshape(made.shape[1:])
            if high + begin + slot < slots:
                made[high + begin + slot] = both[quarter:].reshape(made.shape[1:])
        for first in (begin, high + begin):
            if first < slots:
                copy = pltpu.make_async_copy(
                    made.at[first : first + group], out_ref.at[first : first + group], sems.at[len(copies)]
                )
                copy.start()
                copies.append(copy)
    for copy in copies:
        copy.wait()


def middle_first(count):
    cores = 2
    side = math.isqrt(count // cores)
    half = side // 2
    return [
        ((i // (side * cores) + half) % side * side + (i // cores + half) % side) * cores + cores - 1 - i % cores
        for i in range(count)
    ]


def near(x):
    return pltpu.with_memory_space_constraint(x, pltpu.VMEM)


def far(x):
    return pltpu.with_memory_space_constraint(x, pltpu.HBM)


def exchange(blocks, order):
    count = lax.axis_size("lev")
    moved = {0: blocks[0]}
    for shift in order:
        moved[shift] = lax.ppermute(blocks[shift], "lev", [(i, (i + shift) % count) for i in range(count)])
    return moved


def body(adjoint_grid, lower_diffusion, upper_diffusion, row_lengths, wave_order):
    lev_count = lax.axis_size("lev")
    lat_count = lax.axis_size("lat")
    levels, rows, fields, points = adjoint_grid.shape
    waves = wave_order.shape[0]
    _, _, window = sizes(points, lev_count)
    f32, bf16 = jnp.float32, jnp.bfloat16
    members = levels * fields
    order = sorted(range(lev_count), key=lambda shift: min(shift, lev_count - shift))
    farthest_first = sorted(order[1:], key=lambda shift: -min(shift, lev_count - shift))
    windows = pltpu.VMEM((rows, members, window), bf16)
    made = pl.pallas_call(
        lambda *refs: pack_kernel(lev_count, order, *refs),
        out_shape=[pltpu.VMEM((rows * members, window), bf16)] * lev_count
        + [pltpu.VMEM((rows, LANE), jnp.int32)],
        in_specs=[ANY] * 2,
        out_specs=[VMEM] * (lev_count + 1),
        scratch_shapes=[
            pltpu.VMEM(adjoint_grid.shape, bf16),
            pltpu.SMEM(row_lengths.shape, jnp.int32),
            pltpu.SemaphoreType.DMA((levels + 1,)),
        ],
        name="pack",
        compiler_params=LIMIT,
    )(far(adjoint_grid), far(row_lengths))
    packed = dict(zip(order, made))
    limit = made[-1]
    arrived = exchange(packed, order[1:])
    factor = pltpu.VMEM((lev_count, rows * members, window), f32)
    factors = pl.pallas_call(
        lambda *refs: factor_kernel(lev_count, points, fields, *refs),
        out_shape=[factor] * 3,
        in_specs=[ANY] * 3,
        out_specs=[VMEM] * 3,
        scratch_shapes=[
            pltpu.VMEM(lower_diffusion.shape, f32),
            pltpu.VMEM(upper_diffusion.shape, f32),
            pltpu.SemaphoreType.DMA((2,)),
        ],
        name="factor",
        compiler_params=LIMIT,
        cost_estimate=pl.CostEstimate(flops=10_000_000, bytes_accessed=4_000_000, transcendentals=0),
    )(far(lower_diffusion), far(upper_diffusion), packed[0])
    solved = pl.pallas_call(
        lambda *refs: solve_kernel(lev_count, points, fields, *refs),
        out_shape=[windows] * lev_count,
        in_specs=[VMEM] * (4 + lev_count),
        out_specs=[VMEM] * lev_count,
        scratch_shapes=[
            pltpu.VMEM((lev_count, rows * members, window), f32),
            pltpu.VMEM((lev_count, rows, members, window), f32),
        ],
        name="solve",
        compiler_params=LIMIT,
    )(near(limit), *[near(x) for x in factors], *[near(arrived[shift]) for shift in range(lev_count)])
    returned = exchange(solved, farthest_first)
    fine, coarse = pl.pallas_call(
        table_kernel,
        out_shape=[pltpu.VMEM((rows, DEEP, 2 * waves), bf16), pltpu.VMEM((rows, 2, 24, waves), f32)],
        in_specs=[VMEM, VMEM, ANY],
        out_specs=[VMEM] * 2,
        name="table",
        compiler_params=LIMIT,
        cost_estimate=pl.CostEstimate(flops=10_000_000, bytes_accessed=4_000_000, transcendentals=0),
    )(near(limit), wave_order[None, :], solved[0])
    slots = waves // lat_count
    inner = 4
    high = slots // 2
    early = (0, farthest_first[0])
    members_order = middle_first(lat_count)
    sums = pltpu.VMEM((rows, 2, waves // LANE, members, LANE), f32)
    begun = pl.pallas_call(
        lambda *refs: early_kernel(lev_count, points, early, *refs),
        out_shape=sums,
        in_specs=[VMEM] * (2 + len(early)),
        out_specs=VMEM,
        name="early",
        cost_estimate=pl.CostEstimate(flops=500_000_000, bytes_accessed=4_000_000, transcendentals=0),
        compiler_params=LIMIT,
    )(near(fine), near(coarse), *[near(returned[shift]) for shift in early])
    sent = pl.pallas_call(
        lambda *refs: fourier_kernel(lev_count, points, early, members_order, *refs),
        out_shape=pltpu.VMEM((lat_count, high // inner, inner, LANE), bf16),
        in_specs=[VMEM] * (3 + lev_count),
        out_specs=VMEM,
        scratch_shapes=[sums, pltpu.VMEM((waves, LANE), f32)],
        name="fourier",
        compiler_params=LIMIT,
    )(near(fine), near(coarse), near(begun), *[near(returned[shift]) for shift in range(lev_count)])
    received = lax.all_to_all(
        sent, "lat", split_axis=0, concat_axis=0, tiled=True, axis_index_groups=[members_order]
    )
    return pl.pallas_call(
        lambda *refs: pair_kernel(members_order, *refs),
        out_shape=jax.ShapeDtypeStruct((slots, 2, fields, levels, rows * lat_count), f32),
        in_specs=[VMEM],
        out_specs=ANY,
        scratch_shapes=[
            pltpu.VMEM((lat_count * high, LANE), f32),
            pltpu.VMEM((slots, 2, fields, levels, rows * lat_count), f32),
            pltpu.SemaphoreType.DMA((slots // 4,)),
        ],
        name="pair",
        compiler_params=LIMIT,
    )(near(received))


def solution(mesh):
    in_specs = (P("lev", "lat", None, None), P(None, "lat", "lev"), P(None, "lat", "lev"), P(), P())
    out_specs = P("lat", None, None, "lev", None)
    return jax.shard_map(body, mesh=mesh, in_specs=in_specs, out_specs=out_specs, check_vma=False)
```

profile of v0, /device:TPU:1, one launch (start us, length us, event | category | flops | bytes accessed | tf_op | source)
XLA Modules:
  0.0 35.0 jit_solution(14730217894725145621)
XLA Ops:
  0.0 0.0 copy-start
  0.0 1.2 %pack.1 = (bf16[32,1408]{1,0:T(8,128)(2,1)S(1)}, bf16[32,1408]{1,0:T(8,128)(2,1)S(1)}, bf16[32,1408]{1,0:T(8,128)(2,1)S(1)}, bf16[32,1408]{1,0:T(8,128)(2,1)S(1)}, s32[2,128]{1,0:T(2,128)S(1)}) custom-call(bf16[8,2,2,5136]{3,2,1,0:T(2,128)(2,1)} %refs_0_.2, s32[32]{0:T(128)} %refs_1_.2), custom_call_target="tpu_custom_call" | custom-call | tf_op jit(solution)/shard_map/pack/pallas_call | solution.py:372
  1.2 2.5 %collective-permute-start = (bf16[32,1408]{1,0:T(8,128)(2,1)S(1)}, bf16[32,1408]{1,0:T(8,128)(2,1)S(1)}, u32[]{:S(2)}, u32[]{:S(2)}) collective-permute-start(bf16[32,1408]{1,0:T(8,128)(2,1)S(1)} %get-tuple-element.24), channel_id=1, source_target_pairs={{0,1},{1,2},{2,3},{3,0},{4,5},{5,6},{6,7},{7,4},{8,9},{9,10},{10,1... | collective-permute-start | bytes 270344 | tf_op jit(solution)/shard_map/ppermute | solution.py:357
  3.7 3.3 %collective-permute-start.1 = (bf16[32,1408]{1,0:T(8,128)(2,1)S(1)}, bf16[32,1408]{1,0:T(8,128)(2,1)S(1)}, u32[]{:S(2)}, u32[]{:S(2)}) collective-permute-start(bf16[32,1408]{1,0:T(8,128)(2,1)S(1)} %get-tuple-element.25), channel_id=1, source_target_pairs={{0,2},{1,3},{2,0},{3,1},{4,6},{5,7},{6,4},{7,5},{8,10},{9,11},{10,... | collective-permute-start | bytes 270344 | tf_op jit(solution)/shard_map/ppermute | solution.py:357
  7.0 0.7 %collective-permute-start.2 = (bf16[32,1408]{1,0:T(8,128)(2,1)S(1)}, bf16[32,1408]{1,0:T(8,128)(2,1)S(1)}, u32[]{:S(2)}, u32[]{:S(2)}) collective-permute-start(bf16[32,1408]{1,0:T(8,128)(2,1)S(1)} %get-tuple-element.26), channel_id=1, source_target_pairs={{0,3},{1,0},{2,1},{3,2},{4,7},{5,4},{6,5},{7,6},{8,11},{9,8},{10,9... | collective-permute-start | bytes 270344 | tf_op jit(solution)/shard_map/ppermute | solution.py:357
  7.7 2.7 %factor.1 = (f32[4,32,1408]{2,1,0:T(8,128)S(1)}, f32[4,32,1408]{2,1,0:T(8,128)S(1)}, f32[4,32,1408]{2,1,0:T(8,128)S(1)}) custom-call(f32[32,2,1284]{2,1,0:T(2,128)} %refs_0_.3, f32[32,2,1284]{2,1,0:T(2,128)} %refs_1_.3, bf16[32,1408]{1,0:T(8,128)(2,1)S(1)} %get-tuple-element.20.refs_2_.refs_4_), custom_call_target="tpu_custom_call" | custom-call | flops 10000000 | bytes 4000000 | tf_op jit(solution)/shard_map/factor/pallas_call | solution.py:390
  10.5 0.0 collective-permute-done.refs_5_
  10.5 0.2 collective-permute-done.1.refs_6_
  10.7 0.0 collective-permute-done.2.refs_7_
  10.7 0.7 %solve.1 = (bf16[2,16,1408]{2,1,0:T(8,128)(2,1)S(1)}, bf16[2,16,1408]{2,1,0:T(8,128)(2,1)S(1)}, bf16[2,16,1408]{2,1,0:T(8,128)(2,1)S(1)}, bf16[2,16,1408]{2,1,0:T(8,128)(2,1)S(1)}) custom-call(s32[2,128]{1,0:T(2,128)S(1)} %get-tuple-element.19.refs_0_.limit_ref, f32[4,32,1408]{2,1,0:T(8,128)S(1)} %get-tuple-element.21.refs_1_, ...), custom_call_target="tpu_custom_call" | custom-call | tf_op jit(solution)/shard_map/solve/pallas_call | solution.py:404
  11.4 1.7 %collective-permute-start.3 = (bf16[2,16,1408]{2,1,0:T(8,128)(2,1)S(1)}, bf16[2,16,1408]{2,1,0:T(8,128)(2,1)S(1)}, u32[]{:S(2)}, u32[]{:S(2)}) collective-permute-start(bf16[2,16,1408]{2,1,0:T(8,128)(2,1)S(1)} %get-tuple-element.30), channel_id=1, source_target_pairs={{0,2},{1,3},{2,0},{3,1},{4,6},{5,7},{6,4},{7,5},{8,10},{9,11},{10,... | collective-permute-start | bytes 270344 | tf_op jit(solution)/shard_map/ppermute | solution.py:357
  13.1 1.2 %collective-permute-start.4 = (bf16[2,16,1408]{2,1,0:T(8,128)(2,1)S(1)}, bf16[2,16,1408]{2,1,0:T(8,128)(2,1)S(1)}, u32[]{:S(2)}, u32[]{:S(2)}) collective-permute-start(bf16[2,16,1408]{2,1,0:T(8,128)(2,1)S(1)} %get-tuple-element.31), channel_id=1, source_target_pairs={{0,1},{1,2},{2,3},{3,0},{4,5},{5,6},{6,7},{7,4},{8,9},{9,10},{10,1... | collective-permute-start | bytes 270344 | tf_op jit(solution)/shard_map/ppermute | solution.py:357
  14.3 1.5 %collective-permute-start.5 = (bf16[2,16,1408]{2,1,0:T(8,128)(2,1)S(1)}, bf16[2,16,1408]{2,1,0:T(8,128)(2,1)S(1)}, u32[]{:S(2)}, u32[]{:S(2)}) collective-permute-start(bf16[2,16,1408]{2,1,0:T(8,128)(2,1)S(1)} %get-tuple-element.32), channel_id=1, source_target_pairs={{0,3},{1,0},{2,1},{3,2},{4,7},{5,4},{6,5},{7,6},{8,11},{9,8},{10,9... | collective-permute-start | bytes 270344 | tf_op jit(solution)/shard_map/ppermute | solution.py:357
  15.8 0.0 copy-done
  15.8 1.8 %table.1 = (bf16[2,256,2560]{2,1,0:T(8,128)(2,1)S(1)}, f32[2,2,24,1280]{3,2,1,0:T(8,128)S(1)}) custom-call(s32[2,128]{1,0:T(2,128)S(1)} %get-tuple-element.19.refs_0_.limit_ref, s32[1,1280]{1,0:T(1,128)S(1)} %broadcast_in_dim.3.wave_ref, bf16[2,16,1408]{2,1,0:T(8,128)(2,1)S(1)} %get-tuple-element.27.after_ref.refs_2_.refs_3_), custom_call_target="tpu_custom_call" | custom-call | flops 10000000 | bytes 4000000 | tf_op jit(solution)/shard_map/table/pallas_call | solution.py:417
  17.7 0.0 collective-permute-done.3.refs_3_.refs_5_
  17.7 0.6 %early.1.refs_2_ = f32[2,2,10,16,128]{4,3,2,1,0:T(8,128)S(1)} custom-call(bf16[2,256,2560]{2,1,0:T(8,128)(2,1)S(1)} %get-tuple-element.28.refs_0_, f32[2,2,24,1280]{3,2,1,0:T(8,128)S(1)} %get-tuple-element.29.refs_1_, bf16[2,16,1408]{2,1,0:T(8,128)(2,1)S(1)} %get-tuple-element.27.after_ref.refs_2_.refs_3_, ...), custom_call_target="tpu_custom_call" | custom-call | flops 500000000 | bytes 4000000 | tf_op jit(solution)/shard_map/early/pallas_call | solution.py:432
  18.3 0.0 collective-permute-done.4.refs_4_
  18.3 0.0 collective-permute-done.5.refs_6_
  18.3 1.0 %fourier.1 = bf16[32,5,4,128]{3,2,1,0:T(4,128)(2,1)S(1)} custom-call(bf16[2,256,2560]{2,1,0:T(8,128)(2,1)S(1)} %get-tuple-element.28.refs_0_, f32[2,2,24,1280]{3,2,1,0:T(8,128)S(1)} %get-tuple-element.29.refs_1_, f32[2,2,10,16,128]{4,3,2,1,0:T(8,128)S(1)} %early.1.refs_2_, bf16[2,16,1408]{2,1,0:T(8,128)(2,1)S(1)} %get-tuple-element.27.after_ref.refs_2_.refs_3_, ...), custom_call_target="tpu_custom_call" | custom-call | tf_op jit(solution)/shard_map/fourier/pallas_call | solution.py:441
  19.3 14.5 %all_to_all.5.refs_0_ = bf16[32,5,4,128]{3,2,1,0:T(4,128)(2,1)S(1)} all-to-all(bf16[32,5,4,128]{3,2,1,0:T(4,128)(2,1)S(1)} %fourier.1), channel_id=1, replica_groups={{84,80,92,88,68,64,76,72,116,112,124,120,100,96,108,104,20,16,28,24,4,0..., dimensions={0} | all-to-all | bytes 327680 | tf_op jit(solution)/shard_map/all_to_all | solution.py:450
  33.8 1.2 %pair.1 = f32[40,2,2,8,64]{4,3,2,1,0:T(8,128)} custom-call(bf16[32,5,4,128]{3,2,1,0:T(4,128)(2,1)S(1)} %all_to_all.5.refs_0_), custom_call_target="tpu_custom_call" | custom-call | tf_op jit(solution)/shard_map/pair/pallas_call | solution.py:453
  (1 shorter events, 0.0 us)
Async XLA Ops:
  0.0 15.8 %copy-start = (s32[1280]{0:T(1024)S(1)}, s32[1280]{0:T(1024)}, u32[]{:S(2)}) copy-start(s32[1280]{0:T(1024)} %param.9) | copy-start | bytes 15364
  1.2 9.3 %collective-permute-start = (bf16[32,1408]{1,0:T(8,128)(2,1)S(1)}, bf16[32,1408]{1,0:T(8,128)(2,1)S(1)}, u32[]{:S(2)}, u32[]{:S(2)}) collective-permute-start(bf16[32,1408]{1,0:T(8,128)(2,1)S(1)} %get-tuple-element.24), channel_id=1, source_target_pairs={{0,1},{1,2},{2,3},{3,0},{4,5},{5,6},{6,7},{7,4},{8,9},{9,10},{10,1... | collective-permute-start | bytes 270344 | tf_op jit(solution)/shard_map/ppermute | solution.py:357
  3.7 7.0 %collective-permute-start.1 = (bf16[32,1408]{1,0:T(8,128)(2,1)S(1)}, bf16[32,1408]{1,0:T(8,128)(2,1)S(1)}, u32[]{:S(2)}, u32[]{:S(2)}) collective-permute-start(bf16[32,1408]{1,0:T(8,128)(2,1)S(1)} %get-tuple-element.25), channel_id=1, source_target_pairs={{0,2},{1,3},{2,0},{3,1},{4,6},{5,7},{6,4},{7,5},{8,10},{9,11},{10,... | collective-permute-start | bytes 270344 | tf_op jit(solution)/shard_map/ppermute | solution.py:357
  7.0 3.7 %collective-permute-start.2 = (bf16[32,1408]{1,0:T(8,128)(2,1)S(1)}, bf16[32,1408]{1,0:T(8,128)(2,1)S(1)}, u32[]{:S(2)}, u32[]{:S(2)}) collective-permute-start(bf16[32,1408]{1,0:T(8,128)(2,1)S(1)} %get-tuple-element.26), channel_id=1, source_target_pairs={{0,3},{1,0},{2,1},{3,2},{4,7},{5,4},{6,5},{7,6},{8,11},{9,8},{10,9... | collective-permute-start | bytes 270344 | tf_op jit(solution)/shard_map/ppermute | solution.py:357
  11.4 6.3 %collective-permute-start.3 = (bf16[2,16,1408]{2,1,0:T(8,128)(2,1)S(1)}, bf16[2,16,1408]{2,1,0:T(8,128)(2,1)S(1)}, u32[]{:S(2)}, u32[]{:S(2)}) collective-permute-start(bf16[2,16,1408]{2,1,0:T(8,128)(2,1)S(1)} %get-tuple-element.30), channel_id=1, source_target_pairs={{0,2},{1,3},{2,0},{3,1},{4,6},{5,7},{6,4},{7,5},{8,10},{9,11},{10,... | collective-permute-start | bytes 270344 | tf_op jit(solution)/shard_map/ppermute | solution.py:357
  13.1 5.2 %collective-permute-start.4 = (bf16[2,16,1408]{2,1,0:T(8,128)(2,1)S(1)}, bf16[2,16,1408]{2,1,0:T(8,128)(2,1)S(1)}, u32[]{:S(2)}, u32[]{:S(2)}) collective-permute-start(bf16[2,16,1408]{2,1,0:T(8,128)(2,1)S(1)} %get-tuple-element.31), channel_id=1, source_target_pairs={{0,1},{1,2},{2,3},{3,0},{4,5},{5,6},{6,7},{7,4},{8,9},{9,10},{10,1... | collective-permute-start | bytes 270344 | tf_op jit(solution)/shard_map/ppermute | solution.py:357
  14.3 4.0 %collective-permute-start.5 = (bf16[2,16,1408]{2,1,0:T(8,128)(2,1)S(1)}, bf16[2,16,1408]{2,1,0:T(8,128)(2,1)S(1)}, u32[]{:S(2)}, u32[]{:S(2)}) collective-permute-start(bf16[2,16,1408]{2,1,0:T(8,128)(2,1)S(1)} %get-tuple-element.32), channel_id=1, source_target_pairs={{0,3},{1,0},{2,1},{3,2},{4,7},{5,4},{6,5},{7,6},{8,11},{9,8},{10,9... | collective-permute-start | bytes 270344 | tf_op jit(solution)/shard_map/ppermute | solution.py:357
where the time goes:
time: 35.2 us; the launch traced here: 35 us
  blocking collectives  14.5 us (41%)
  starting transfers between devices  11 us (31%)
  Pallas kernels  9.26 us (26%)
    all_to_all x1, blocking collectives, body(): lax.all_to_all(sent, 'lat', split_axis=0, concat_axis=0, tiled=True, axis...  14.5 us
    ppermute x6, starting transfers between devices, exchange(): lax.ppermute(blocks[shift], 'lev', [(i, (i + shift) % count) for i in ran...  11 us
    pallas_call x1, Pallas kernels, body(): pl.pallas_call(lambda *refs: factor_kernel(lev_count, points, fields, *re...  2.72 us
    pallas_call x1, Pallas kernels, body(): pl.pallas_call(table_kernel, out_shape=[pltpu.VMEM((rows, DEEP, 2 * waves...  1.84 us
    pallas_call x1, Pallas kernels, body(): pl.pallas_call(lambda *refs: pair_kernel(members_order, *refs), out_shape...  1.24 us
    pallas_call x1, Pallas kernels, body(): pl.pallas_call(lambda *refs: pack_kernel(lev_count, order, *refs), out_sh...  1.16 us
    pallas_call x1, Pallas kernels, body(): pl.pallas_call(lambda *refs: fourier_kernel(lev_count, points, early, mem...  0.97 us
    pallas_call x1, Pallas kernels, body(): pl.pallas_call(lambda *refs: solve_kernel(lev_count, points, fields, *ref...  0.75 us
  transfers between devices with their start and end apart: 6, of which 1 were waited for; matrix products, arithmetic and copies ran while one was open for 0% of the time, Pallas kernels for 15%

commit v1 on v0

--- a/solution.py
+++ b/solution.py
@@ -213,7 +213,7 @@
 
 def early_kernel(lev_count, points, shifts, fine_ref, coarse_ref, *refs):
     _, step, _ = sizes(points, lev_count)
-    sources, spectra = refs[:-1], refs[-1]
+    sources, begun, spectra = refs[: len(shifts)], refs[len(shifts) : -1], refs[-1]
     rows, _, _, members, _ = spectra.shape
     waves = fine_ref.shape[2] // 2
     per = step // DEEP
@@ -223,8 +223,11 @@
             [source[row, :, DEEP * a : DEEP * (a + 1)] for source in sources for a in range(1, per)], axis=0
         )
         for tile in range(waves // DEEP):
-            zero = jnp.zeros((members, DEEP), jnp.float32)
-            sums = blocks_sum(fine_ref, coarse_ref, row, tile, main, places, zero, zero)
+            halves = [tile * (DEEP // LANE) + half for half in range(DEEP // LANE)]
+            before = [jnp.zeros((members, DEEP), jnp.float32)] * 2
+            for ref in begun:
+                before = [jnp.concatenate([ref[row, part, at] for at in halves], axis=1) for part in range(2)]
+            sums = blocks_sum(fine_ref, coarse_ref, row, tile, main, places, *before)
             for half in range(DEEP // LANE):
                 for part, value in enumerate(sums):
                     spectra[row, part, tile * (DEEP // LANE) + half] = value[:, LANE * half : LANE * (half + 1)]
@@ -426,18 +429,23 @@
     slots = waves // lat_count
     inner = 4
     high = slots // 2
-    early = (0, farthest_first[0])
     members_order = middle_first(lat_count)
     sums = pltpu.VMEM((rows, 2, waves // LANE, members, LANE), f32)
-    begun = pl.pallas_call(
-        lambda *refs: early_kernel(lev_count, points, early, *refs),
-        out_shape=sums,
-        in_specs=[VMEM] * (2 + len(early)),
-        out_specs=VMEM,
-        name="early",
-        cost_estimate=pl.CostEstimate(flops=500_000_000, bytes_accessed=4_000_000, transcendentals=0),
-        compiler_params=LIMIT,
-    )(near(fine), near(coarse), *[near(returned[shift]) for shift in early])
+    begun = []
+    for ready in ((0, farthest_first[0]), farthest_first[1:2]):
+        begun = [
+            pl.pallas_call(
+                lambda *refs, ready=ready: early_kernel(lev_count, points, ready, *refs),
+                out_shape=sums,
+                in_specs=[VMEM] * (2 + len(ready) + len(begun)),
+                out_specs=VMEM,
+                name="early",
+                cost_estimate=pl.CostEstimate(flops=500_000_000, bytes_accessed=4_000_000, transcendentals=0),
+                compiler_params=LIMIT,
+            )(near(fine), near(coarse), *[near(returned[shift]) for shift in ready], *[near(x) for x in begun])
+        ]
+    begun = begun[0]
+    early = (0, *farthest_first[:2])
     sent = pl.pallas_call(
         lambda *refs: fourier_kernel(lev_count, points, early, members_order, *refs),
         out_shape=pltpu.VMEM((lat_count, high // inner, inner, LANE), bf16),

time: 35.2 us -> 35.7 us (1.014)
  Pallas kernels: 9.26 us -> 9.69 us
    pallas_call x1 -> x2, Pallas kernels: 0.58 us -> 1.17 us  [body(): pl.pallas_call(lambda *refs, ready=ready: early_kernel(lev_count, points,...]
  transfers between devices with their start and end apart: 6 -> 6, of which waited for: 1 -> 1; matrix products, arithmetic and copies ran while one was open for 0% -> 0% of each run, Pallas kernels for 15% -> 16%
where the time goes in v1:
time: 35.7 us; the launch traced here: 35.5 us
  blocking collectives  14.4 us (40%)
  starting transfers between devices  11 us (31%)
  Pallas kernels  9.69 us (27%)
    all_to_all x1, blocking collectives, body(): lax.all_to_all(sent, 'lat', split_axis=0, concat_axis=0, tiled=True, axis...  14.4 us
    ppermute x6, starting transfers between devices, exchange(): lax.ppermute(blocks[shift], 'lev', [(i, (i + shift) % count) for i in ran...  11 us
    pallas_call x1, Pallas kernels, body(): pl.pallas_call(lambda *refs: factor_kernel(lev_count, points, fields, *re...  2.72 us
    pallas_call x1, Pallas kernels, body(): pl.pallas_call(table_kernel, out_shape=[pltpu.VMEM((rows, DEEP, 2 * waves...  1.84 us
    pallas_call x1, Pallas kernels, body(): pl.pallas_call(lambda *refs: pair_kernel(members_order, *refs), out_shape...  1.24 us
    pallas_call x2, Pallas kernels, body(): pl.pallas_call(lambda *refs, ready=ready: early_kernel(lev_count, points,...  1.17 us
    pallas_call x1, Pallas kernels, body(): pl.pallas_call(lambda *refs: pack_kernel(lev_count, order, *refs), out_sh...  1.16 us
    pallas_call x1, Pallas kernels, body(): pl.pallas_call(lambda *refs: fourier_kernel(lev_count, points, early, mem...  0.81 us
  transfers between devices with their start and end apart: 6, of which 1 were waited for; matrix products, arithmetic and copies ran while one was open for 0% of the time, Pallas kernels for 16%

profile of v1, /device:TPU:1, one launch (start us, length us, event | category | flops | bytes accessed | tf_op | source)
XLA Modules:
  0.0 35.5 jit_solution(12226666395715743565)
XLA Ops:
  0.0 0.0 copy-start
  0.0 1.2 %pack.1 = (bf16[32,1408]{1,0:T(8,128)(2,1)S(1)}, bf16[32,1408]{1,0:T(8,128)(2,1)S(1)}, bf16[32,1408]{1,0:T(8,128)(2,1)S(1)}, bf16[32,1408]{1,0:T(8,128)(2,1)S(1)}, s32[2,128]{1,0:T(2,128)S(1)}) custom-call(bf16[8,2,2,5136]{3,2,1,0:T(2,128)(2,1)} %refs_0_.2, s32[32]{0:T(128)} %refs_1_.2), custom_call_target="tpu_custom_call" | custom-call | tf_op jit(solution)/shard_map/pack/pallas_call | solution.py:375
  1.2 2.5 %collective-permute-start = (bf16[32,1408]{1,0:T(8,128)(2,1)S(1)}, bf16[32,1408]{1,0:T(8,128)(2,1)S(1)}, u32[]{:S(2)}, u32[]{:S(2)}) collective-permute-start(bf16[32,1408]{1,0:T(8,128)(2,1)S(1)} %get-tuple-element.24), channel_id=1, source_target_pairs={{0,1},{1,2},{2,3},{3,0},{4,5},{5,6},{6,7},{7,4},{8,9},{9,10},{10,1... | collective-permute-start | bytes 270344 | tf_op jit(solution)/shard_map/ppermute | solution.py:360
  3.7 3.3 %collective-permute-start.1 = (bf16[32,1408]{1,0:T(8,128)(2,1)S(1)}, bf16[32,1408]{1,0:T(8,128)(2,1)S(1)}, u32[]{:S(2)}, u32[]{:S(2)}) collective-permute-start(bf16[32,1408]{1,0:T(8,128)(2,1)S(1)} %get-tuple-element.25), channel_id=1, source_target_pairs={{0,2},{1,3},{2,0},{3,1},{4,6},{5,7},{6,4},{7,5},{8,10},{9,11},{10,... | collective-permute-start | bytes 270344 | tf_op jit(solution)/shard_map/ppermute | solution.py:360
  7.0 0.7 %collective-permute-start.2 = (bf16[32,1408]{1,0:T(8,128)(2,1)S(1)}, bf16[32,1408]{1,0:T(8,128)(2,1)S(1)}, u32[]{:S(2)}, u32[]{:S(2)}) collective-permute-start(bf16[32,1408]{1,0:T(8,128)(2,1)S(1)} %get-tuple-element.26), channel_id=1, source_target_pairs={{0,3},{1,0},{2,1},{3,2},{4,7},{5,4},{6,5},{7,6},{8,11},{9,8},{10,9... | collective-permute-start | bytes 270344 | tf_op jit(solution)/shard_map/ppermute | solution.py:360
  7.7 2.7 %factor.1 = (f32[4,32,1408]{2,1,0:T(8,128)S(1)}, f32[4,32,1408]{2,1,0:T(8,128)S(1)}, f32[4,32,1408]{2,1,0:T(8,128)S(1)}) custom-call(f32[32,2,1284]{2,1,0:T(2,128)} %refs_0_.3, f32[32,2,1284]{2,1,0:T(2,128)} %refs_1_.3, bf16[32,1408]{1,0:T(8,128)(2,1)S(1)} %get-tuple-element.20.refs_2_.refs_4_), custom_call_target="tpu_custom_call" | custom-call | flops 10000000 | bytes 4000000 | tf_op jit(solution)/shard_map/factor/pallas_call | solution.py:393
  10.5 0.0 collective-permute-done.refs_5_
  10.5 0.2 collective-permute-done.1.refs_6_
  10.7 0.0 collective-permute-done.2.refs_7_
  10.7 0.7 %solve.1 = (bf16[2,16,1408]{2,1,0:T(8,128)(2,1)S(1)}, bf16[2,16,1408]{2,1,0:T(8,128)(2,1)S(1)}, bf16[2,16,1408]{2,1,0:T(8,128)(2,1)S(1)}, bf16[2,16,1408]{2,1,0:T(8,128)(2,1)S(1)}) custom-call(s32[2,128]{1,0:T(2,128)S(1)} %get-tuple-element.19.refs_0_.limit_ref, f32[4,32,1408]{2,1,0:T(8,128)S(1)} %get-tuple-element.21.refs_1_, ...), custom_call_target="tpu_custom_call" | custom-call | tf_op jit(solution)/shard_map/solve/pallas_call | solution.py:407
  11.4 1.7 %collective-permute-start.4 = (bf16[2,16,1408]{2,1,0:T(8,128)(2,1)S(1)}, bf16[2,16,1408]{2,1,0:T(8,128)(2,1)S(1)}, u32[]{:S(2)}, u32[]{:S(2)}) collective-permute-start(bf16[2,16,1408]{2,1,0:T(8,128)(2,1)S(1)} %get-tuple-element.31), channel_id=1, source_target_pairs={{0,2},{1,3},{2,0},{3,1},{4,6},{5,7},{6,4},{7,5},{8,10},{9,11},{10,... | collective-permute-start | bytes 270344 | tf_op jit(solution)/shard_map/ppermute | solution.py:360
  13.1 1.2 %collective-permute-start.3 = (bf16[2,16,1408]{2,1,0:T(8,128)(2,1)S(1)}, bf16[2,16,1408]{2,1,0:T(8,128)(2,1)S(1)}, u32[]{:S(2)}, u32[]{:S(2)}) collective-permute-start(bf16[2,16,1408]{2,1,0:T(8,128)(2,1)S(1)} %get-tuple-element.30), channel_id=1, source_target_pairs={{0,1},{1,2},{2,3},{3,0},{4,5},{5,6},{6,7},{7,4},{8,9},{9,10},{10,1... | collective-permute-start | bytes 270344 | tf_op jit(solution)/shard_map/ppermute | solution.py:360
  14.3 0.0 copy-done
  14.3 1.6 %collective-permute-start.5 = (bf16[2,16,1408]{2,1,0:T(8,128)(2,1)S(1)}, bf16[2,16,1408]{2,1,0:T(8,128)(2,1)S(1)}, u32[]{:S(2)}, u32[]{:S(2)}) collective-permute-start(bf16[2,16,1408]{2,1,0:T(8,128)(2,1)S(1)} %get-tuple-element.32), channel_id=1, source_target_pairs={{0,3},{1,0},{2,1},{3,2},{4,7},{5,4},{6,5},{7,6},{8,11},{9,8},{10,9... | collective-permute-start | bytes 270344 | tf_op jit(solution)/shard_map/ppermute | solution.py:360
  15.9 1.8 %table.1 = (bf16[2,256,2560]{2,1,0:T(8,128)(2,1)S(1)}, f32[2,2,24,1280]{3,2,1,0:T(8,128)S(1)}) custom-call(s32[2,128]{1,0:T(2,128)S(1)} %get-tuple-element.19.refs_0_.limit_ref, s32[1,1280]{1,0:T(1,128)S(1)} %broadcast_in_dim.3.wave_ref, bf16[2,16,1408]{2,1,0:T(8,128)(2,1)S(1)} %get-tuple-element.27.after_ref.refs_2_.refs_3_), custom_call_target="tpu_custom_call" | custom-call | flops 10000000 | bytes 4000000 | tf_op jit(solution)/shard_map/table/pallas_call | solution.py:420
  17.8 0.0 collective-permute-done.4.refs_3_.refs_5_
  17.8 0.6 %early.2.refs_3_ = f32[2,2,10,16,128]{4,3,2,1,0:T(8,128)S(1)} custom-call(bf16[2,256,2560]{2,1,0:T(8,128)(2,1)S(1)} %get-tuple-element.28.refs_0_, f32[2,2,24,1280]{3,2,1,0:T(8,128)S(1)} %get-tuple-element.29.refs_1_, bf16[2,16,1408]{2,1,0:T(8,128)(2,1)S(1)} %get-tuple-element.27.after_ref.refs_2_.refs_3_, ...), custom_call_target="tpu_custom_call" | custom-call | flops 500000000 | bytes 4000000 | tf_op jit(solution)/shard_map/early/pallas_call | solution.py:437
  18.4 0.0 collective-permute-done.3.refs_2_.refs_4_
  18.4 0.6 %early.3.refs_2_ = f32[2,2,10,16,128]{4,3,2,1,0:T(8,128)S(1)} custom-call(bf16[2,256,2560]{2,1,0:T(8,128)(2,1)S(1)} %get-tuple-element.28.refs_0_, f32[2,2,24,1280]{3,2,1,0:T(8,128)S(1)} %get-tuple-element.29.refs_1_, bf16[2,16,1408]{2,1,0:T(8,128)(2,1)S(1)} %collective-permute-done.3.refs_2_.refs_4_, f32[2,2,10,16,128]{4,3,2,1,0:T(8,128)S(1)} %early.2.refs_3_), custom_call_target="tpu_custom_call" | custom-call | flops 500000000 | bytes 4000000 | tf_op jit(solution)/shard_map/early/pallas_call | solution.py:437
  19.0 0.0 collective-permute-done.5.refs_6_
  19.0 0.8 %fourier.1 = bf16[32,5,4,128]{3,2,1,0:T(4,128)(2,1)S(1)} custom-call(bf16[2,256,2560]{2,1,0:T(8,128)(2,1)S(1)} %get-tuple-element.28.refs_0_, f32[2,2,24,1280]{3,2,1,0:T(8,128)S(1)} %get-tuple-element.29.refs_1_, f32[2,2,10,16,128]{4,3,2,1,0:T(8,128)S(1)} %early.3.refs_2_, bf16[2,16,1408]{2,1,0:T(8,128)(2,1)S(1)} %get-tuple-element.27.after_ref.refs_2_.refs_3_, ...), custom_call_target="tpu_custom_call" | custom-call | tf_op jit(solution)/shard_map/fourier/pallas_call | solution.py:449
  19.8 14.4 %all_to_all.5.refs_0_ = bf16[32,5,4,128]{3,2,1,0:T(4,128)(2,1)S(1)} all-to-all(bf16[32,5,4,128]{3,2,1,0:T(4,128)(2,1)S(1)} %fourier.1), channel_id=1, replica_groups={{84,80,92,88,68,64,76,72,116,112,124,120,100,96,108,104,20,16,28,24,4,0..., dimensions={0} | all-to-all | bytes 327680 | tf_op jit(solution)/shard_map/all_to_all | solution.py:458
  34.2 1.2 %pair.1 = f32[40,2,2,8,64]{4,3,2,1,0:T(8,128)} custom-call(bf16[32,5,4,128]{3,2,1,0:T(4,128)(2,1)S(1)} %all_to_all.5.refs_0_), custom_call_target="tpu_custom_call" | custom-call | tf_op jit(solution)/shard_map/pair/pallas_call | solution.py:461
  (1 shorter events, 0.0 us)
Async XLA Ops:
  0.0 14.3 %copy-start = (s32[1280]{0:T(1024)S(1)}, s32[1280]{0:T(1024)}, u32[]{:S(2)}) copy-start(s32[1280]{0:T(1024)} %param.9) | copy-start | bytes 15364
  1.2 9.3 %collective-permute-start = (bf16[32,1408]{1,0:T(8,128)(2,1)S(1)}, bf16[32,1408]{1,0:T(8,128)(2,1)S(1)}, u32[]{:S(2)}, u32[]{:S(2)}) collective-permute-start(bf16[32,1408]{1,0:T(8,128)(2,1)S(1)} %get-tuple-element.24), channel_id=1, source_target_pairs={{0,1},{1,2},{2,3},{3,0},{4,5},{5,6},{6,7},{7,4},{8,9},{9,10},{10,1... | collective-permute-start | bytes 270344 | tf_op jit(solution)/shard_map/ppermute | solution.py:360
  3.7 7.0 %collective-permute-start.1 = (bf16[32,1408]{1,0:T(8,128)(2,1)S(1)}, bf16[32,1408]{1,0:T(8,128)(2,1)S(1)}, u32[]{:S(2)}, u32[]{:S(2)}) collective-permute-start(bf16[32,1408]{1,0:T(8,128)(2,1)S(1)} %get-tuple-element.25), channel_id=1, source_target_pairs={{0,2},{1,3},{2,0},{3,1},{4,6},{5,7},{6,4},{7,5},{8,10},{9,11},{10,... | collective-permute-start | bytes 270344 | tf_op jit(solution)/shard_map/ppermute | solution.py:360
  7.0 3.7 %collective-permute-start.2 = (bf16[32,1408]{1,0:T(8,128)(2,1)S(1)}, bf16[32,1408]{1,0:T(8,128)(2,1)S(1)}, u32[]{:S(2)}, u32[]{:S(2)}) collective-permute-start(bf16[32,1408]{1,0:T(8,128)(2,1)S(1)} %get-tuple-element.26), channel_id=1, source_target_pairs={{0,3},{1,0},{2,1},{3,2},{4,7},{5,4},{6,5},{7,6},{8,11},{9,8},{10,9... | collective-permute-start | bytes 270344 | tf_op jit(solution)/shard_map/ppermute | solution.py:360
  11.4 6.3 %collective-permute-start.4 = (bf16[2,16,1408]{2,1,0:T(8,128)(2,1)S(1)}, bf16[2,16,1408]{2,1,0:T(8,128)(2,1)S(1)}, u32[]{:S(2)}, u32[]{:S(2)}) collective-permute-start(bf16[2,16,1408]{2,1,0:T(8,128)(2,1)S(1)} %get-tuple-element.31), channel_id=1, source_target_pairs={{0,2},{1,3},{2,0},{3,1},{4,6},{5,7},{6,4},{7,5},{8,10},{9,11},{10,... | collective-permute-start | bytes 270344 | tf_op jit(solution)/shard_map/ppermute | solution.py:360
  13.1 5.2 %collective-permute-start.3 = (bf16[2,16,1408]{2,1,0:T(8,128)(2,1)S(1)}, bf16[2,16,1408]{2,1,0:T(8,128)(2,1)S(1)}, u32[]{:S(2)}, u32[]{:S(2)}) collective-permute-start(bf16[2,16,1408]{2,1,0:T(8,128)(2,1)S(1)} %get-tuple-element.30), channel_id=1, source_target_pairs={{0,1},{1,2},{2,3},{3,0},{4,5},{5,6},{6,7},{7,4},{8,9},{9,10},{10,1... | collective-permute-start | bytes 270344 | tf_op jit(solution)/shard_map/ppermute | solution.py:360
  14.3 4.7 %collective-permute-start.5 = (bf16[2,16,1408]{2,1,0:T(8,128)(2,1)S(1)}, bf16[2,16,1408]{2,1,0:T(8,128)(2,1)S(1)}, u32[]{:S(2)}, u32[]{:S(2)}) collective-permute-start(bf16[2,16,1408]{2,1,0:T(8,128)(2,1)S(1)} %get-tuple-element.32), channel_id=1, source_target_pairs={{0,3},{1,0},{2,1},{3,2},{4,7},{5,4},{6,5},{7,6},{8,11},{9,8},{10,9... | collective-permute-start | bytes 270344 | tf_op jit(solution)/shard_map/ppermute | solution.py:360
